TPU v7x, 32 devices: a whole 2x2x4 slice. The times are simulated.
32 devices in a mesh: pipe: 4 (over x, core), seq: 8 (over z, y).
Axes of the slice: x: 2, y: 2, z: 4, core: 2. Of those that a mesh axis runs over, the one named last changes fastest.
Arguments:
- value_in: bfloat16 [4, 1024, 4096], P('pipe', 'seq'), may hold values from -6 to 6
- gate_one: bfloat16 [4, 1024, 4096], P('pipe', 'seq'), may hold values from -6 to 6
- gate_two: bfloat16 [4, 1024, 4096], P('pipe', 'seq'), may hold values from -6 to 6
- out_grad: bfloat16 [4, 1024, 4096], P('pipe', 'seq'), may hold values from -6 to 6
- w_embed: float32 [4, 33, 64], P('pipe'), may hold values from -1 to 1
- b_embed: float32 [4, 64], P('pipe'), may hold values from -4 to 4
- w_filter: float32 [4, 64, 4096], P('pipe', None, 'seq'), may hold values from -0.75 to 0.75
- decay: float32 [4, 4096], P('pipe', 'seq'), may hold values from 0.3 to 128
- skip: float32 [4, 4096], P('pipe', 'seq'), may hold values from -4 to 4
Outputs:
- next_input: bfloat16 [4, 1024, 4096], P('pipe', 'seq')
- grad_value: bfloat16 [4, 1024, 4096], P('pipe', 'seq')
- grad_gate_one: bfloat16 [4, 1024, 4096], P('pipe', 'seq')
- grad_gate_two: bfloat16 [4, 1024, 4096], P('pipe', 'seq')
- grad_w_embed: float32 [4, 33, 64], P('pipe')
- grad_b_embed: float32 [4, 64], P('pipe')
- grad_w_filter: float32 [4, 64, 4096], P('pipe', None, 'seq')
- grad_decay: float32 [4, 4096], P('pipe', 'seq')
- grad_skip: float32 [4, 4096], P('pipe', 'seq')
All inputs are finite; a program needn't handle non-finite values.
Results may differ from a plain program's by a relative error of at most 0.0058.
Values may be sent and summed in bfloat16 or wider, within the bound.
A program may use at most 128 MiB of HBM per device.

v0:
```python
import math
import jax
import jax.numpy as jnp
from jax import lax
from jax.sharding import PartitionSpec as P

E = 33


def from_behind(value, axis, steps):
    count = lax.axis_size(axis)
    pairs = [(source, (source + steps) % count) for source in range(count)]
    return lax.ppermute(value, axis, pairs)


def contract(form, left, right):
    return jnp.einsum(form, left, right, precision=lax.Precision.HIGHEST)


def position_features(length):
    position_ids = jnp.arange(length, dtype=jnp.int32)
    band_count = (E - 1) // 2
    band_index = jnp.arange(1, band_count + 1, dtype=jnp.int32)
    turn_ids = band_index[:, None] * band_index[:, None] * position_ids[None, :] % length
    angles = 2.0 * math.pi / length * turn_ids.astype(jnp.float32)
    position_ramp = position_ids.astype(jnp.float32)[None, :] / length
    return jnp.concatenate([position_ramp, jnp.cos(angles), jnp.sin(angles)], axis=0)


def build_tables(length):
    fft_total = 2 * length
    outer_len = 128
    half_len = outer_len // 2
    kept_len = half_len + 1
    inner_len = fft_total // outer_len
    index_kept = jnp.arange(kept_len, dtype=jnp.int32)
    index_half = jnp.arange(half_len, dtype=jnp.int32)
    index_inner = jnp.arange(inner_len, dtype=jnp.int32)
    angle_outer = (
        2.0
        * math.pi
        / outer_len
        * (index_kept[:, None] * index_half[None, :] % outer_len).astype(jnp.float32)
    )
    cos_outer = jnp.cos(angle_outer)
    sin_outer = jnp.sin(angle_outer)
    table_first = jnp.concatenate([cos_outer, -sin_outer], axis=0)
    angle_twist = (
        2.0
        * math.pi
        / fft_total
        * (index_kept[:, None] * index_inner[None, :] % fft_total).astype(jnp.float32)
    )
    cos_twist = jnp.cos(angle_twist)[:, :, None]
    sin_twist = jnp.sin(angle_twist)[:, :, None]
    angle_inner = (
        2.0
        * math.pi
        / inner_len
        * (index_inner[:, None] * index_inner[None, :] % inner_len).astype(jnp.float32)
    )
    cos_inner = jnp.cos(angle_inner)
    sin_inner = jnp.sin(angle_inner)
    table_second = jnp.stack(
        [jnp.stack([cos_inner, sin_inner], axis=1), jnp.stack([-sin_inner, cos_inner], axis=1)],
        axis=0,
    )
    table_back = jnp.stack(
        [jnp.stack([cos_inner, -sin_inner], axis=1), jnp.stack([sin_inner, cos_inner], axis=1)],
        axis=0,
    )
    weight_kept = (
        jnp.where((index_kept == 0) | (index_kept == half_len), 1.0, 2.0).astype(jnp.float32)
        / fft_total
    )
    table_last = jnp.stack(
        [
            jnp.transpose(cos_outer) * weight_kept[None, :],
            -jnp.transpose(sin_outer) * weight_kept[None, :],
        ],
        axis=1,
    )
    return (
        table_first,
        cos_twist,
        sin_twist,
        table_second,
        table_back,
        table_last,
        half_len,
        kept_len,
        inner_len,
    )


def staged_forward(field, tables_all):
    (
        table_first,
        cos_twist,
        sin_twist,
        table_second,
        table_back,
        table_last,
        half_len,
        kept_len,
        inner_len,
    ) = tables_all
    columns = field.shape[1]
    shaped = field.reshape(half_len, inner_len, columns)
    stacked = contract("kn,npc->kpc", table_first, shaped)
    part_re = stacked[:kept_len]
    part_im = stacked[kept_len:]
    twisted = jnp.stack(
        [part_re * cos_twist + part_im * sin_twist, part_im * cos_twist - part_re * sin_twist],
        axis=0,
    )
    return contract("sqrp,rkpc->skqc", table_second, twisted)


def staged_inverse(spec, tables_all):
    (
        table_first,
        cos_twist,
        sin_twist,
        table_second,
        table_back,
        table_last,
        half_len,
        kept_len,
        inner_len,
    ) = tables_all
    columns = spec.shape[3]
    sectioned = contract("sprq,rkqc->skpc", table_back, spec)
    section_re = sectioned[0]
    section_im = sectioned[1]
    twisted = jnp.stack(
        [
            section_re * cos_twist - section_im * sin_twist,
            section_im * cos_twist + section_re * sin_twist,
        ],
        axis=0,
    )
    result = contract("nrk,rkpc->npc", table_last, twisted)
    return result.reshape(half_len * inner_len, columns)


def dense_tables(length):
    block = 128
    fine = jnp.arange(block, dtype=jnp.int32)
    coarse = jnp.arange(length // block, dtype=jnp.int32) * block
    point = jnp.arange(length, dtype=jnp.int32)
    unit = math.pi / (2 * length)

    def pair(count):
        angle = unit * (count % (4 * length)).astype(jnp.float32)
        return (jnp.cos(angle), jnp.sin(angle))

    def joined(first, second):
        (cos_f, sin_f), (cos_s, sin_s) = (first, second)
        cos_j = cos_s[:, None, :] * cos_f[None] - sin_s[:, None, :] * sin_f[None]
        sin_j = sin_s[:, None, :] * cos_f[None] + cos_s[:, None, :] * sin_f[None]
        return (cos_j.reshape(length, length), sin_j.reshape(length, length))

    odd = 2 * point + 1
    cos_k, sin_k = joined(
        pair((2 * fine + 1)[:, None] * point[None, :]), pair((2 * coarse)[:, None] * point[None, :])
    )
    ahead = jnp.concatenate([cos_k, -sin_k], axis=0).astype(jnp.bfloat16)
    cos_n, sin_n = joined(pair(fine[:, None] * odd[None, :]), pair(coarse[:, None] * odd[None, :]))
    back = (jnp.concatenate([cos_n, -sin_n], axis=1) * (1.0 / length)).astype(jnp.bfloat16)
    return (ahead, back)


def dense_forward(field, tables_all):
    spec = jnp.dot(tables_all[0], field.astype(jnp.bfloat16), preferred_element_type=jnp.float32)
    return spec.reshape(2, field.shape[0], field.shape[1])


def dense_inverse(spec, tables_all):
    flat = spec.reshape(2 * spec.shape[1], spec.shape[2])
    return jnp.dot(tables_all[1], flat.astype(jnp.bfloat16), preferred_element_type=jnp.float32)


def spectral_product(left, right, conjugate_left):
    left_re = left[0]
    left_im = left[1]
    right_re = right[0]
    right_im = right[1]
    if conjugate_left:
        left_im = -left_im
    return jnp.stack(
        [left_re * right_re - left_im * right_im, left_re * right_im + left_im * right_re], axis=0
    )


def per_device(value_in, gate_one, gate_two, out_grad, w_embed, b_embed, w_filter, decay, skip):
    values = value_in[0]
    gate_first = gate_one[0]
    gate_second = gate_two[0]
    cotangent = out_grad[0]
    filter_w = w_filter[0]
    shards = lax.axis_size("seq")
    length = values.shape[0] * shards
    weighted = (values.astype(jnp.float32) * gate_first.astype(jnp.float32)).astype(jnp.bfloat16)
    upstream = (cotangent.astype(jnp.float32) * gate_second.astype(jnp.float32)).astype(
        jnp.bfloat16
    )
    features = position_features(length)
    preact = contract("ef,et->ft", w_embed[0], features) + b_embed[0][:, None]
    activation = jnp.sin(preact)
    positions = jnp.arange(length, dtype=jnp.int32).astype(jnp.float32)[:, None]
    envelope = jnp.exp(-decay[0][None, :] * positions / length) * (1.0 / math.sqrt(length))
    kernel = contract("ft,fc->tc", activation, filter_w) * envelope
    if length <= 1024 and length % 128 == 0:
        tables_all = dense_tables(length)
        forward_transform, inverse_transform = (dense_forward, dense_inverse)
    else:
        tables_all = build_tables(length)
        forward_transform, inverse_transform = (staged_forward, staged_inverse)
    kernel_spec = forward_transform(kernel, tables_all)
    skip_row = skip[0][None, :]
    weighted_chan, upstream_chan = (
        lax.all_to_all(weighted, "seq", split_axis=1, concat_axis=0, tiled=True),
        lax.all_to_all(upstream, "seq", split_axis=1, concat_axis=0, tiled=True),
    )
    weighted_f = weighted_chan.astype(jnp.float32)
    weighted_spec = forward_transform(weighted_f, tables_all)
    conv = inverse_transform(spectral_product(kernel_spec, weighted_spec, False), tables_all)
    mixed_chan, weighted_f, weighted_spec = (
        (conv + skip_row * weighted_f).astype(jnp.bfloat16),
        weighted_f,
        weighted_spec,
    )
    upstream_f = upstream_chan.astype(jnp.float32)
    upstream_spec = forward_transform(upstream_f, tables_all)
    backward_conv = inverse_transform(
        spectral_product(kernel_spec, upstream_spec, True), tables_all
    )
    grad_chan = (backward_conv + skip_row * upstream_f).astype(jnp.bfloat16)
    grad_skip = jnp.sum(upstream_f * weighted_f, axis=0)
    grad_kernel = inverse_transform(
        spectral_product(weighted_spec, upstream_spec, True), tables_all
    )
    grad_chan, grad_skip, grad_kernel = (grad_chan, grad_skip, grad_kernel)
    mixed_seq, grad_weighted = (
        lax.all_to_all(mixed_chan, "seq", split_axis=0, concat_axis=1, tiled=True),
        lax.all_to_all(grad_chan, "seq", split_axis=0, concat_axis=1, tiled=True),
    )
    output = (gate_second.astype(jnp.float32) * mixed_seq.astype(jnp.float32)).astype(jnp.bfloat16)
    next_input = from_behind(output, "pipe", 1)
    grad_decay = jnp.sum(grad_kernel * kernel * (-positions / length), axis=0)
    grad_raw = grad_kernel * envelope
    grad_filter_w = contract("ft,tc->fc", activation, grad_raw)
    grad_preact = contract("fc,tc->ft", filter_w, grad_raw) * jnp.cos(preact)
    part_weight = contract("et,ft->ef", features, grad_preact)
    part_bias = jnp.sum(grad_preact, axis=1)
    grad_embed_w, grad_embed_b = lax.psum((part_weight, part_bias), "seq")
    grad_values = (grad_weighted.astype(jnp.float32) * gate_first.astype(jnp.float32)).astype(
        jnp.bfloat16
    )
    grad_first = (grad_weighted.astype(jnp.float32) * values.astype(jnp.float32)).astype(
        jnp.bfloat16
    )
    grad_second = (cotangent.astype(jnp.float32) * mixed_seq.astype(jnp.float32)).astype(
        jnp.bfloat16
    )
    moved_values, moved_first, moved_second = from_behind(
        (grad_values, grad_first, grad_second), "pipe", -1
    )
    return (
        next_input[None],
        moved_values[None],
        moved_first[None],
        moved_second[None],
        grad_embed_w[None],
        grad_embed_b[None],
        grad_filter_w[None],
        grad_decay[None],
        grad_skip[None],
    )


def solution(mesh):
    return jax.shard_map(
        per_device,
        mesh=mesh,
        in_specs=(
            P("pipe", "seq", None),
            P("pipe", "seq", None),
            P("pipe", "seq", None),
            P("pipe", "seq", None),
            P("pipe", None, None),
            P("pipe", None),
            P("pipe", None, "seq"),
            P("pipe", "seq"),
            P("pipe", "seq"),
        ),
        out_specs=(
            P("pipe", "seq", None),
            P("pipe", "seq", None),
            P("pipe", "seq", None),
            P("pipe", "seq", None),
            P("pipe", None, None),
            P("pipe", None),
            P("pipe", None, "seq"),
            P("pipe", "seq"),
            P("pipe", "seq"),
        ),
        check_vma=False,
    )
```

profile of v0, /device:TPU:0, one launch (start us, length us, event | category | flops | bytes accessed | tf_op | source)
XLA Modules:
  0.0 202.9 jit_solution(786132404300499328)
XLA Ops:
  0.7 1.8 fusion.10
  2.5 0.4 copy.27
  2.9 1.3 copy.20
  4.2 7.3 %all-to-all-start.2 = ((bf16[128,8,512]{2,0,1:T(8,128)(2,1)}), bf16[128,8,512]{2,0,1:T(8,128)(2,1)S(1)}, u32[]{:S(2)}, u32[]{:S(2)}) async-start(bf16[128,8,512]{2,0,1:T(8,128)(2,1)} %copy.20), calls=%async_computation.2 | async-start | bytes 2097152 | tf_op jit(solution)/shard_map/all_to_all | solution.py:224
  12.2 0.4 copy.26
  12.6 1.3 copy.18
  14.3 0.3 fusion.72
  14.7 1.9 fusion.95
  16.6 3.2 %fusion.54 = (f32[128,1024]{1,0:T(8,128)}, f32[128,1024]{1,0:T(8,128)}) fusion(s32[128]{0:T(128)S(1)} %multiply_add_fusion.1), kind=kLoop, calls=%fused_computation.84 | loop fusion | flops 1835008 | bytes 1049088 | tf_op jit(solution)/shard_map/cos | solution.py:156
  19.8 2.0 %fusion.56 = (f32[128,1024]{1,0:T(8,128)S(1)}, f32[128,1024]{1,0:T(8,128)S(1)}) fusion(s32[1024]{0:T(1024)S(1)} %multiply_add_fusion), kind=kLoop, calls=%fused_computation.86 | loop fusion | flops 1835008 | bytes 1052672 | tf_op jit(solution)/shard_map/cos | solution.py:156
  21.8 3.5 %fusion.12 = f32[1024,512]{1,0:T(8,128)} fusion(f32[1024,64]{0,1:T(8,128)S(1)} %get-tuple-element.46, f32[1024]{0:T(1024)S(1)} %iota_convert_fusion, f32[512]{0:T(512)S(1)} %bitcast.129, f32[1,64,512]{2,1,0:T(8,128)S(1)} %copy-done), kind=kOutput, calls=%fused_computation.40 | convolution fusion | flops 404750336 | bytes 2496512 | tf_op jit(solution)/shard_map/ft,fc->tc/dot_general | solution.py:17
  25.3 11.9 %all-to-all-done.2 = bf16[128,8,512]{2,0,1:T(8,128)(2,1)S(1)} async-done(((bf16[128,8,512]{2,0,1:T(8,128)(2,1)}), bf16[128,8,512]{2,0,1:T(8,128)(2,1)S(1)}, u32[]{:S(2)}, u32[]{:S(2)}) %all-to-all-start.2) | async-done | bytes 1048608 | tf_op jit(solution)/shard_map/all_to_all | solution.py:224
  37.2 3.7 %all-to-all-start = ((bf16[128,8,512]{2,0,1:T(8,128)(2,1)}), bf16[128,8,512]{2,0,1:T(8,128)(2,1)S(1)}, u32[]{:S(2)}, u32[]{:S(2)}) async-start(bf16[128,8,512]{2,0,1:T(8,128)(2,1)} %copy.18), calls=%async_computation | async-start | bytes 2097152 | tf_op jit(solution)/shard_map/all_to_all | solution.py:223
  41.0 2.4 %subtract_convert_fusion = (bf16[8,128,1024]{2,1,0:T(8,128)(2,1)S(1)}, bf16[8,128,1024]{2,1,0:T(8,128)(2,1)S(1)}) fusion(f32[128,1024]{1,0:T(8,128)} %get-tuple-element.45, f32[8,1024]{1,0:T(8,128)S(1)} %get-tuple-element.43, f32[128,1024]{1,0:T(8,128)} %get-tuple-element.44, f32[8,1024]{1,0:T(8,128)S(1)} %get-tuple-element.42), kind=kLoop, calls=%fused_computation.4 | loop fusion | flops 9437184 | bytes 5308416 | tf_op jit(solution)/shard_map/convert.23
  43.5 4.5 %multiply_subtract_fusion = (f32[8,128,1024]{2,1,0:T(8,128)}, f32[8,128,1024]{2,1,0:T(8,128)}) fusion(f32[128,1024]{1,0:T(8,128)S(1)} %get-tuple-element.39, f32[8,1024]{1,0:T(8,128)S(1)} %get-tuple-element.37, f32[128,1024]{1,0:T(8,128)S(1)} %get-tuple-element.38, f32[8,1024]{1,0:T(8,128)S(1)} %get-tuple-element.36), kind=kLoop, calls=%fused_computation.6 | loop fusion | flops 7340032 | bytes 9502720 | tf_op jit(solution)/shard_map/sub | solution.py:160
  47.9 4.4 %fusion.19 = f32[2048,512]{1,0:T(8,128)} fusion(bf16[1024,1024]{1,0:T(8,128)(2,1)S(1)} %bitcast.122, bf16[1024,1024]{1,0:T(8,128)(2,1)S(1)} %bitcast.119, f32[1024,512]{1,0:T(8,128)S(1)} %copy-done.28), kind=kOutput, calls=%fused_computation.45 | convolution fusion | flops 2156396544 | bytes 10485760 | tf_op jit(solution)/shard_map/dot_general | solution.py:175
  52.3 4.5 %fusion.17 = f32[2048,512]{1,0:T(8,128)} fusion(bf16[1024,512]{1,0:T(8,128)(2,1)S(1)} %bitcast.111, bf16[1024,1024]{1,0:T(8,128)(2,1)S(1)} %bitcast.123, bf16[1024,1024]{1,0:T(8,128)(2,1)S(1)} %bitcast.120), kind=kOutput, calls=%fused_computation.43 | convolution fusion | flops 2155872256 | bytes 9437184 | tf_op jit(solution)/shard_map/dot_general | solution.py:175
  56.8 10.1 %all-to-all-done = bf16[128,8,512]{2,0,1:T(8,128)(2,1)S(1)} async-done(((bf16[128,8,512]{2,0,1:T(8,128)(2,1)}), bf16[128,8,512]{2,0,1:T(8,128)(2,1)S(1)}, u32[]{:S(2)}, u32[]{:S(2)}) %all-to-all-start) | async-done | bytes 1048608 | tf_op jit(solution)/shard_map/all_to_all | solution.py:223
  66.8 5.0 %fusion.18 = f32[2048,512]{1,0:T(8,128)S(1)} fusion(bf16[1024,512]{1,0:T(8,128)(2,1)S(1)} %bitcast.113, bf16[1024,1024]{1,0:T(8,128)(2,1)} %bitcast.124, bf16[1024,1024]{1,0:T(8,128)(2,1)} %bitcast.121), kind=kOutput, calls=%fused_computation.44 | convolution fusion | flops 2155872256 | bytes 9437184 | tf_op jit(solution)/shard_map/dot_general | solution.py:175
  71.9 1.9 fusion.30
  73.9 1.7 pad_maximum_fusion.1
  75.6 1.2 copy-done.3
  76.8 1.3 copy-done.6
  78.1 3.3 %add_convert_fusion.3 = bf16[1024,512]{1,0:T(8,128)(2,1)} fusion(bf16[1024,512]{1,0:T(8,128)(2,1)S(1)} %bitcast.114, bf16[2048,512]{1,0:T(8,128)(2,1)S(1)} %bitcast.125, f32[512]{0:T(512)S(1)} %bitcast.134, f32[1024,1024]{1,0:T(8,128)S(1)} %bitcast.106, f32[1024,1024]{1,0:T(8,128)S(1)} %bitcast.103), kind=kOutput, calls=%fused_computation.35 | convolution fusion | flops 2155872256 | bytes 12584960 | tf_op jit(solution)/shard_map/dot_general | solution.py:181
  81.4 3.8 %all-to-all-start.1 = ((bf16[8,128,512]{2,1,0:T(8,128)(2,1)}), bf16[8,128,512]{2,1,0:T(8,128)(2,1)S(1)}, u32[]{:S(2)}, u32[]{:S(2)}) async-start(bf16[8,128,512]{2,1,0:T(8,128)(2,1)} %bitcast.15), calls=%async_computation.1 | async-start | bytes 2097152 | tf_op jit(solution)/shard_map/all_to_all | solution.py:246
  85.2 4.8 %fusion.28 = (bf16[1,1024,512]{2,1,0:T(8,128)(2,1)S(1)}, bf16[1,1024,512]{2,1,0:T(8,128)(2,1)S(1)}) fusion(f32[2048,512]{1,0:T(8,128)} %fusion.17, f32[2048,512]{1,0:T(8,128)} %fusion.19), kind=kLoop, calls=%fused_computation.52 | loop fusion | flops 4718592 | bytes 10485760 | tf_op jit(solution)/shard_map/stack | solution.py:191
  90.2 2.0 copy-done.4
  92.2 3.3 %add_convert_fusion.1 = bf16[1024,512]{1,0:T(8,128)(2,1)} fusion(bf16[1024,512]{1,0:T(8,128)(2,1)S(1)} %bitcast.112, bf16[2048,512]{1,0:T(8,128)(2,1)S(1)} %bitcast.117, f32[512]{0:T(512)S(1)} %bitcast.135, f32[1024,1024]{1,0:T(8,128)S(1)} %bitcast.107, f32[1024,1024]{1,0:T(8,128)S(1)} %bitcast.104), kind=kOutput, calls=%fused_computation.32 | convolution fusion | flops 2155872256 | bytes 12584960 | tf_op jit(solution)/shard_map/dot_general | solution.py:181
  95.5 15.5 %all-to-all-done.1 = bf16[8,128,512]{2,1,0:T(8,128)(2,1)S(1)} async-done(((bf16[8,128,512]{2,1,0:T(8,128)(2,1)}), bf16[8,128,512]{2,1,0:T(8,128)(2,1)S(1)}, u32[]{:S(2)}, u32[]{:S(2)}) %all-to-all-start.1) | async-done | bytes 1048608 | tf_op jit(solution)/shard_map/all_to_all | solution.py:246
  111.0 3.6 %all-to-all-start.3 = ((bf16[8,128,512]{2,1,0:T(8,128)(2,1)}), bf16[8,128,512]{2,1,0:T(8,128)(2,1)S(1)}, u32[]{:S(2)}, u32[]{:S(2)}) async-start(bf16[8,128,512]{2,1,0:T(8,128)(2,1)} %bitcast.127), calls=%async_computation.3 | async-start | bytes 2097152 | tf_op jit(solution)/shard_map/all_to_all | solution.py:247
  115.1 1.0 copy-done.11
  116.4 1.9 fusion.7
  118.3 22.3 %all-to-all-done.3 = bf16[8,128,512]{2,1,0:T(8,128)(2,1)S(1)} async-done(((bf16[8,128,512]{2,1,0:T(8,128)(2,1)}), bf16[8,128,512]{2,1,0:T(8,128)(2,1)S(1)}, u32[]{:S(2)}, u32[]{:S(2)}) %all-to-all-start.3) | async-done | bytes 1048608 | tf_op jit(solution)/shard_map/all_to_all | solution.py:247
  141.1 0.7 copy-done.14
  142.1 1.9 fusion.2
  143.9 1.6 collective-permute-start.1
  145.6 0.5 collective-permute-start
  146.1 4.4 %multiply_reduce_fusion.1 = (f32[512]{0:T(512)}, f32[1024,512]{1,0:T(8,128)S(1)}) fusion(f32[1024,512]{1,0:T(8,128)} %fusion.12, f32[1024]{0:T(1024)S(1)} %negate_multiply_fusion, bf16[2048,512]{1,0:T(8,128)(2,1)S(1)} %bitcast.118, f32[1024,1024]{1,0:T(8,128)S(1)} %bitcast.108, f32[1024,1024]{1,0:T(8,128)S(1)} %bitcast.105), kind=kOutput, calls=%fused_computation.29 | convolution fusion | flops 2155347456 | bytes 14686208 | tf_op jit(solution)/shard_map/dot_general | solution.py:181
  150.5 3.3 %fusion.96 = (f32[64]{0:T(128)S(1)}, f32[1024,64]{0,1:T(8,128)S(1)}) fusion(f32[1024,64]{0,1:T(8,128)S(1)} %copy-done.21, f32[1,64,512]{2,1,0:T(8,128)S(1)} %copy-done, f32[1024,512]{1,0:T(8,128)S(1)} %get-tuple-element.51, f32[1024]{0:T(1024)S(1)} %iota_convert_fusion, f32[512]{0:T(512)S(1)} %bitcast.130), kind=kOutput, calls=%fused_computation.143 | convolution fusion | flops 404881344 | bytes 2758912 | tf_op jit(solution)/shard_map/fc,tc->ft/dot_general | solution.py:17
  153.9 0.4 convolution_bitcast_fusion
  154.2 35.7 %all-reduce = (f32[1,33,64]{2,1,0:T(8,128)S(1)}, f32[1,64]{1,0:T(1,128)}) all-reduce(f32[1,33,64]{2,1,0:T(8,128)S(1)} %convolution_bitcast_fusion, f32[1,64]{1,0:T(1,128)S(1)} %bitcast.133), channel_id=1, replica_groups=mesh['pipe'=4,'seq'=8] {'seq'}, use_global_device_ids=true, to_apply=%region_0.1 | all-reduce | flops 2176 | bytes 17408 | tf_op jit(solution)/shard_map/psum | solution.py:257
  190.0 0.6 copy.22
  190.6 1.0 multiply_reduce_fusion
  191.5 3.4 %fusion.23 = f32[1,64,512]{2,1,0:T(8,128)} fusion(f32[1024,64]{0,1:T(8,128)} %copy-done.20, f32[1024,512]{1,0:T(8,128)S(1)} %copy-done.27, f32[1024]{0:T(1024)S(1)} %iota_convert_fusion, f32[512]{0:T(512)S(1)} %bitcast.131), kind=kOutput, calls=%fused_computation.48 | convolution fusion | flops 404750336 | bytes 2496512 | tf_op jit(solution)/shard_map/ft,tc->fc/dot_general | solution.py:17
  195.0 2.3 %copy.38 = bf16[1,128,4096]{2,1,0:T(8,128)(2,1)} copy(bf16[1,128,4096]{2,1,0:T(8,128)(2,1)} %bitcast.17) | data formatting | bytes 2097152
  197.3 2.3 %copy.39 = bf16[1,128,4096]{2,1,0:T(8,128)(2,1)} copy(bf16[1,128,4096]{2,1,0:T(8,128)(2,1)} %bitcast.27) | data formatting | bytes 2097152
  199.6 1.0 copy.40
  200.6 2.3 %copy.41 = bf16[1,128,4096]{2,1,0:T(8,128)(2,1)} copy(bf16[1,128,4096]{2,1,0:T(8,128)(2,1)} %bitcast.31) | data formatting | bytes 2097152
  (76 shorter events, 3.2 us)
Async XLA Ops:
  0.6 21.2 %copy-start = (f32[1,64,512]{2,1,0:T(8,128)S(1)}, f32[1,64,512]{2,1,0:T(8,128)}, u32[]{:S(2)}) copy-start(f32[1,64,512]{2,1,0:T(8,128)} %param.15) | copy-start | bytes 393220
  2.9 8.6 %copy-start.13 = (bf16[1,128,4096]{2,1,0:T(8,128)(2,1)S(1)}, bf16[1,128,4096]{2,1,0:T(8,128)(2,1)}, u32[]{:S(2)}) copy-start(bf16[1,128,4096]{2,1,0:T(8,128)(2,1)} %param.10) | copy-start | bytes 3145732
  2.9 8.6 %copy-start.15 = (bf16[1,128,4096]{2,1,0:T(8,128)(2,1)S(1)}, bf16[1,128,4096]{2,1,0:T(8,128)(2,1)}, u32[]{:S(2)}) copy-start(bf16[1,128,4096]{2,1,0:T(8,128)(2,1)} %param.9) | copy-start | bytes 3145732
  4.2 33.0 %all-to-all-start.2 = ((bf16[128,8,512]{2,0,1:T(8,128)(2,1)}), bf16[128,8,512]{2,0,1:T(8,128)(2,1)S(1)}, u32[]{:S(2)}, u32[]{:S(2)}) async-start(bf16[128,8,512]{2,0,1:T(8,128)(2,1)} %copy.20), calls=%async_computation.2 | async-start | bytes 2097152 | tf_op jit(solution)/shard_map/all_to_all | solution.py:224
  11.5 0.7 copy-start.23
  12.2 2.5 %copy-start.22 = (f32[1,33,64]{2,0,1:T(1,128)S(1)}, f32[1,33,64]{2,0,1:T(1,128)}, u32[]{:S(2)}) copy-start(f32[1,33,64]{2,0,1:T(1,128)} %param.13) | copy-start | bytes 25348
  12.2 2.5 %copy-start.24 = (f32[1,64]{1,0:T(1,128)S(1)}, f32[1,64]{1,0:T(1,128)}, u32[]{:S(2)}) copy-start(f32[1,64]{1,0:T(1,128)} %param.14) | copy-start | bytes 772
  16.6 5.3 %copy-start.20 = (f32[1024,64]{0,1:T(8,128)}, f32[1024,64]{0,1:T(8,128)S(1)}, u32[]{:S(2)}) copy-start(f32[1024,64]{0,1:T(8,128)S(1)} %get-tuple-element.46) | copy-start | bytes 786436
  37.2 29.6 %all-to-all-start = ((bf16[128,8,512]{2,0,1:T(8,128)(2,1)}), bf16[128,8,512]{2,0,1:T(8,128)(2,1)S(1)}, u32[]{:S(2)}, u32[]{:S(2)}) async-start(bf16[128,8,512]{2,0,1:T(8,128)(2,1)} %copy.18), calls=%async_computation | async-start | bytes 2097152 | tf_op jit(solution)/shard_map/all_to_all | solution.py:223
  43.4 8.9 %copy-start.18 = (bf16[8,128,1024]{2,1,0:T(8,128)(2,1)}, bf16[8,128,1024]{2,1,0:T(8,128)(2,1)S(1)}, u32[]{:S(2)}) copy-start(bf16[8,128,1024]{2,1,0:T(8,128)(2,1)S(1)} %get-tuple-element.34) | copy-start | bytes 6291460
  43.4 8.9 %copy-start.19 = (bf16[8,128,1024]{2,1,0:T(8,128)(2,1)}, bf16[8,128,1024]{2,1,0:T(8,128)(2,1)S(1)}, u32[]{:S(2)}) copy-start(bf16[8,128,1024]{2,1,0:T(8,128)(2,1)S(1)} %get-tuple-element.35) | copy-start | bytes 6291460
  43.4 4.5 %copy-start.28 = (f32[1024,512]{1,0:T(8,128)S(1)}, f32[1024,512]{1,0:T(8,128)}, u32[]{:S(2)}) copy-start(f32[1024,512]{1,0:T(8,128)} %fusion.12) | copy-start | bytes 6291460
  66.8 8.8 %copy-start.9 = (bf16[128,8,512]{2,0,1:T(8,128)(2,1)}, bf16[128,8,512]{2,0,1:T(8,128)(2,1)S(1)}, u32[]{:S(2)}) copy-start(bf16[128,8,512]{2,0,1:T(8,128)(2,1)S(1)} %all-to-all-done) | copy-start | bytes 3145732
  66.8 5.0 %copy-start.1 = (f32[2048,512]{1,0:T(8,128)S(1)}, f32[2048,512]{1,0:T(8,128)}, u32[]{:S(2)}) copy-start(f32[2048,512]{1,0:T(8,128)} %fusion.19) | copy-start | bytes 12582916
  66.8 5.1 %copy-start.2 = (f32[2048,512]{1,0:T(8,128)S(1)}, f32[2048,512]{1,0:T(8,128)}, u32[]{:S(2)}) copy-start(f32[2048,512]{1,0:T(8,128)} %fusion.17) | copy-start | bytes 12582916
  73.9 2.9 %copy-start.3 = (f32[8,128,1024]{2,1,0:T(8,128)S(1)}, f32[8,128,1024]{2,1,0:T(8,128)}, u32[]{:S(2)}) copy-start(f32[8,128,1024]{2,1,0:T(8,128)} %get-tuple-element.32) | copy-start | bytes 12582916
  73.9 4.2 %copy-start.6 = (f32[8,128,1024]{2,1,0:T(8,128)S(1)}, f32[8,128,1024]{2,1,0:T(8,128)}, u32[]{:S(2)}) copy-start(f32[8,128,1024]{2,1,0:T(8,128)} %get-tuple-element.33) | copy-start | bytes 12582916
  73.9 4.2 %copy-start.25 = (f32[1,512]{1,0:T(1,128)S(1)}, f32[1,512]{1,0:T(1,128)}, u32[]{:S(2)}) copy-start(f32[1,512]{1,0:T(1,128)} %param.17) | copy-start | bytes 6148
  81.4 29.6 %all-to-all-start.1 = ((bf16[8,128,512]{2,1,0:T(8,128)(2,1)}), bf16[8,128,512]{2,1,0:T(8,128)(2,1)S(1)}, u32[]{:S(2)}, u32[]{:S(2)}) async-start(bf16[8,128,512]{2,1,0:T(8,128)(2,1)} %bitcast.15), calls=%async_computation.1 | async-start | bytes 2097152 | tf_op jit(solution)/shard_map/all_to_all | solution.py:246
  85.2 5.0 %copy-start.7 = (f32[8,128,1024]{2,1,0:T(8,128)S(1)}, f32[8,128,1024]{2,1,0:T(8,128)}, u32[]{:S(2)}) copy-start(f32[8,128,1024]{2,1,0:T(8,128)} %get-tuple-element.33) | copy-start | bytes 12582916
  90.0 2.2 %copy-start.4 = (f32[8,128,1024]{2,1,0:T(8,128)S(1)}, f32[8,128,1024]{2,1,0:T(8,128)}, u32[]{:S(2)}) copy-start(f32[8,128,1024]{2,1,0:T(8,128)} %get-tuple-element.32) | copy-start | bytes 12582916
  111.0 29.5 %all-to-all-start.3 = ((bf16[8,128,512]{2,1,0:T(8,128)(2,1)}), bf16[8,128,512]{2,1,0:T(8,128)(2,1)S(1)}, u32[]{:S(2)}, u32[]{:S(2)}) async-start(bf16[8,128,512]{2,1,0:T(8,128)(2,1)} %bitcast.127), calls=%async_computation.3 | async-start | bytes 2097152 | tf_op jit(solution)/shard_map/all_to_all | solution.py:247
  114.9 1.2 copy-start.11
  114.9 1.5 copy-start.12
  140.5 1.2 copy-start.14
  140.5 1.5 copy-start.16
  140.8 5.2 %copy-start.8 = (f32[8,128,1024]{2,1,0:T(8,128)S(1)}, f32[8,128,1024]{2,1,0:T(8,128)}, u32[]{:S(2)}) copy-start(f32[8,128,1024]{2,1,0:T(8,128)} %get-tuple-element.33) | copy-start | bytes 12582916
  142.1 4.0 %copy-start.5 = (f32[8,128,1024]{2,1,0:T(8,128)S(1)}, f32[8,128,1024]{2,1,0:T(8,128)}, u32[]{:S(2)}) copy-start(f32[8,128,1024]{2,1,0:T(8,128)} %get-tuple-element.32) | copy-start | bytes 12582916
  142.1 4.0 %copy-start.17 = (bf16[2,1024,512]{2,1,0:T(8,128)(2,1)S(1)}, bf16[2,1024,512]{2,1,0:T(8,128)(2,1)}, u32[]{:S(2)}) copy-start(bf16[2,1024,512]{2,1,0:T(8,128)(2,1)} %get-tuple-element.53) | copy-start | bytes 6291460
  143.9 51.1 %collective-permute-start.2 = (bf16[128,4096]{1,0:T(8,128)(2,1)}, bf16[128,4096]{1,0:T(8,128)(2,1)S(1)}, u32[]{:S(2)}, u32[]{:S(2)}) collective-permute-start(bf16[128,4096]{1,0:T(8,128)(2,1)} %get-tuple-element.30), channel_id=1, source_target_pairs={{0,24},{8,0},{16,8},{24,16},{1,25},{9,1},{17,9},{25,17},{2,26},{10... | collective-permute-start | bytes 3145736 | tf_op jit(solution)/shard_map/ppermute | solution.py:13
  143.9 51.1 %collective-permute-start.1 = (bf16[128,4096]{1,0:T(8,128)(2,1)}, bf16[128,4096]{1,0:T(8,128)(2,1)}, u32[]{:S(2)}, u32[]{:S(2)}) collective-permute-start(bf16[128,4096]{1,0:T(8,128)(2,1)} %get-tuple-element.31), channel_id=1, source_target_pairs={{0,24},{8,0},{16,8},{24,16},{1,25},{9,1},{17,9},{25,17},{2,26},{10... | collective-permute-start | bytes 3145736 | tf_op jit(solution)/shard_map/ppermute | solution.py:13
  145.5 49.5 %collective-permute-start.3 = (bf16[128,4096]{1,0:T(8,128)(2,1)}, bf16[128,4096]{1,0:T(8,128)(2,1)}, u32[]{:S(2)}, u32[]{:S(2)}) collective-permute-start(bf16[128,4096]{1,0:T(8,128)(2,1)} %get-tuple-element.28), channel_id=1, source_target_pairs={{0,24},{8,0},{16,8},{24,16},{1,25},{9,1},{17,9},{25,17},{2,26},{10... | collective-permute-start | bytes 3145736 | tf_op jit(solution)/shard_map/ppermute | solution.py:13
  145.6 49.4 %collective-permute-start = (bf16[128,4096]{1,0:T(8,128)(2,1)}, bf16[128,4096]{1,0:T(8,128)(2,1)}, u32[]{:S(2)}, u32[]{:S(2)}) collective-permute-start(bf16[128,4096]{1,0:T(8,128)(2,1)} %get-tuple-element.29), channel_id=1, source_target_pairs={{0,8},{8,16},{16,24},{24,0},{1,9},{9,17},{17,25},{25,1},{2,10},{10... | collective-permute-start | bytes 3145736 | tf_op jit(solution)/shard_map/ppermute | solution.py:13
  146.1 4.4 %copy-start.21 = (f32[1024,64]{0,1:T(8,128)S(1)}, f32[1024,64]{0,1:T(8,128)}, u32[]{:S(2)}) copy-start(f32[1024,64]{0,1:T(8,128)} %get-tuple-element.47) | copy-start | bytes 786436
  150.5 3.7 %copy-start.26 = (f32[1024,512]{1,0:T(8,128)}, f32[1024,512]{1,0:T(8,128)S(1)}, u32[]{:S(2)}) copy-start(f32[1024,512]{1,0:T(8,128)S(1)} %get-tuple-element.51) | copy-start | bytes 6291460
  150.5 40.1 %copy-start.10 = (bf16[128,8,512]{2,0,1:T(8,128)(2,1)S(1)}, bf16[128,8,512]{2,0,1:T(8,128)(2,1)}, u32[]{:S(2)}) copy-start(bf16[128,8,512]{2,0,1:T(8,128)(2,1)} %copy-done.9) | copy-start | bytes 3145732
  189.9 1.6 copy-start.27
where the time goes:
time: 204 us; the launch traced here: 203 us
  waiting for transfers between devices  59.8 us (29%)
  matrix products  37.4 us (18%)
  blocking collectives  35.7 us (18%)
  other arithmetic  28.9 us (14%)
  starting transfers between devices  20.5 us (10%)
  local copies, waits for them, and re-layouts  19.6 us (10%)
    psum x1, blocking collectives, per_device(): grad_embed_w, grad_embed_b = lax.psum((part_weight, part_bias), 'seq')  35.7 us
    all_to_all x1, waiting for transfers between devices, per_device(): lax.all_to_all(grad_chan, 'seq', split_axis=0, concat_axis=1, tiled=True)  22.3 us
    unnamed x65, local copies, waits for them, and re-layouts  16.6 us
    all_to_all x1, waiting for transfers between devices, per_device(): lax.all_to_all(mixed_chan, 'seq', split_axis=0, concat_axis=1, tiled=True)  15.5 us
    dot_general x3, matrix products, dense_forward(): jnp.dot(tables_all[0], field.astype(jnp.bfloat16), preferred_element_type...  13.8 us
    dot_general x5, matrix products, contract(): return jnp.einsum(form, left, right, precision=lax.Precision.HIGHEST)  12.5 us
    all_to_all x1, waiting for transfers between devices, per_device(): lax.all_to_all(upstream, 'seq', split_axis=1, concat_axis=0, tiled=True)  11.9 us
    dot_general x3, matrix products, dense_inverse(): jnp.dot(tables_all[1], flat.astype(jnp.bfloat16), preferred_element_type=...  11 us
  transfers between devices with their start and end apart: 8, of which 4 were waited for; matrix products, arithmetic and copies ran while one was open for 26% of the time, Pallas kernels for 0%

commit v1 on v0

--- a/solution.py
+++ b/solution.py
@@ -243,7 +243,12 @@
     )
     grad_chan, grad_skip, grad_kernel = (grad_chan, grad_skip, grad_kernel)
     mixed_seq, grad_weighted = (
-        lax.all_to_all(mixed_chan, "seq", split_axis=0, concat_axis=1, tiled=True),
+        jnp.concatenate(
+            lax.all_to_all(
+                jnp.stack(jnp.split(mixed_chan, lax.axis_size("seq"), axis=0)), "seq", 0, 0
+            ),
+            axis=1,
+        ),
         lax.all_to_all(grad_chan, "seq", split_axis=0, concat_axis=1, tiled=True),
     )
     output = (gate_second.astype(jnp.float32) * mixed_seq.astype(jnp.float32)).astype(jnp.bfloat16)

time: 204 us -> 218 us (1.069)
  local copies, waits for them, and re-layouts: 19.6 us -> 32 us
  waiting for transfers between devices: 59.8 us -> 54.6 us
  other arithmetic: 28.9 us -> 31.9 us
  matrix products: 37.4 us -> 40 us
    all_to_all x1, waiting for transfers between devices: 22.3 us -> 13.2 us  [per_device(): lax.all_to_all(grad_chan, 'seq', split_axis=0, concat_axis=1, tiled=True)]
    unnamed x65, local copies, waits for them, and re-layouts: 16.6 us -> 24.7 us
    all_to_all x1, waiting for transfers between devices: 15.5 us -> 21.9 us  [per_device(): lax.all_to_all(jnp.stack(jnp.split(mixed_chan, lax.axis_size('seq'), axis...]
    another operation x4, other arithmetic: 8.64 us -> 5.35 us  [spectral_product(): jnp.stack([left_re * right_re - left_im * right_im, left_re * right_im +...]
    convert_element_type x0 -> x1, other arithmetic: none -> 2.88 us  [per_device(): mixed_seq.astype(jnp.float32)]
    convert_element_type x1, local copies, waits for them, and re-layouts: 0.17 us -> 2.9 us  [per_device(): mixed_seq.astype(jnp.float32)]
    dot_general x3, matrix products: 11 us -> 13.7 us  [dense_inverse(): jnp.dot(tables_all[1], flat.astype(jnp.bfloat16), preferred_element_type=...]
  transfers between devices with their start and end apart: 8 -> 8, of which waited for: 4 -> 4; matrix products, arithmetic and copies ran while one was open for 26% -> 31% of each run, Pallas kernels for 0% -> 0%
where the time goes in v1:
time: 218 us; the launch traced here: 217 us
  waiting for transfers between devices  54.6 us (25%)
  matrix products  40 us (18%)
  blocking collectives  36.3 us (17%)
  local copies, waits for them, and re-layouts  32 us (15%)
  other arithmetic  31.9 us (15%)
  starting transfers between devices  21.6 us (10%)
    psum x1, blocking collectives, per_device(): grad_embed_w, grad_embed_b = lax.psum((part_weight, part_bias), 'seq')  36.3 us
    unnamed x65, local copies, waits for them, and re-layouts  24.7 us
    all_to_all x1, waiting for transfers between devices, per_device(): lax.all_to_all(jnp.stack(jnp.split(mixed_chan, lax.axis_size('seq'), axis...  21.9 us
    dot_general x3, matrix products, dense_forward(): jnp.dot(tables_all[0], field.astype(jnp.bfloat16), preferred_element_type...  13.8 us
    dot_general x3, matrix products, dense_inverse(): jnp.dot(tables_all[1], flat.astype(jnp.bfloat16), preferred_element_type=...  13.7 us
    all_to_all x1, waiting for transfers between devices, per_device(): lax.all_to_all(grad_chan, 'seq', split_axis=0, concat_axis=1, tiled=True)  13.2 us
    dot_general x5, matrix products, contract(): return jnp.einsum(form, left, right, precision=lax.Precision.HIGHEST)  12.6 us
    all_to_all x1, waiting for transfers between devices, per_device(): lax.all_to_all(upstream, 'seq', split_axis=1, concat_axis=0, tiled=True)  9.81 us
  transfers between devices with their start and end apart: 8, of which 4 were waited for; matrix products, arithmetic and copies ran while one was open for 31% of the time, Pallas kernels for 0%

profile of v1, /device:TPU:0, one launch (start us, length us, event | category | flops | bytes accessed | tf_op | source)
XLA Modules:
  0.0 217.4 jit_solution(6561853705585109339)
XLA Ops:
  0.7 1.7 copy.22
  3.3 1.3 copy.26
  4.7 7.3 %all-to-all-start.2 = ((bf16[128,8,512]{2,0,1:T(8,128)(2,1)}), bf16[128,8,512]{2,0,1:T(8,128)(2,1)S(1)}, u32[]{:S(2)}, u32[]{:S(2)}) async-start(bf16[128,8,512]{2,0,1:T(8,128)(2,1)} %copy.26), calls=%async_computation.2 | async-start | bytes 2097152 | tf_op jit(solution)/shard_map/all_to_all | solution.py:224
  12.0 1.8 fusion.3
  14.3 1.3 copy.23
  16.4 1.9 fusion.103
  18.3 3.2 %fusion.54 = (f32[128,1024]{1,0:T(8,128)}, f32[128,1024]{1,0:T(8,128)}) fusion(s32[128]{0:T(128)S(1)} %multiply_add_fusion.1), kind=kLoop, calls=%fused_computation.84 | loop fusion | flops 1835008 | bytes 1049088 | tf_op jit(solution)/shard_map/cos | solution.py:156
  21.5 2.9 %fusion.56 = (f32[128,1024]{1,0:T(8,128)}, f32[128,1024]{1,0:T(8,128)}) fusion(s32[1024]{0:T(1024)S(1)} %multiply_add_fusion), kind=kLoop, calls=%fused_computation.86 | loop fusion | flops 1835008 | bytes 1052672 | tf_op jit(solution)/shard_map/cos | solution.py:156
  24.4 3.5 %fusion.12 = f32[1024,512]{1,0:T(8,128)} fusion(f32[1024,64]{0,1:T(8,128)S(1)} %get-tuple-element.55, f32[1024]{0:T(1024)S(1)} %iota_convert_fusion, f32[512]{0:T(512)S(1)} %bitcast.156, f32[1,64,512]{2,1,0:T(8,128)S(1)} %copy-done), kind=kOutput, calls=%fused_computation.40 | convolution fusion | flops 404750336 | bytes 2496512 | tf_op jit(solution)/shard_map/ft,fc->tc/dot_general | solution.py:17
  27.9 9.8 %all-to-all-done.2 = bf16[128,8,512]{2,0,1:T(8,128)(2,1)S(1)} async-done(((bf16[128,8,512]{2,0,1:T(8,128)(2,1)}), bf16[128,8,512]{2,0,1:T(8,128)(2,1)S(1)}, u32[]{:S(2)}, u32[]{:S(2)}) %all-to-all-start.2) | async-done | bytes 1048608 | tf_op jit(solution)/shard_map/all_to_all | solution.py:224
  37.7 4.4 %all-to-all-start = ((bf16[128,8,512]{2,0,1:T(8,128)(2,1)}), bf16[128,8,512]{2,0,1:T(8,128)(2,1)}, u32[]{:S(2)}, u32[]{:S(2)}) async-start(bf16[128,8,512]{2,0,1:T(8,128)(2,1)} %copy.23), calls=%async_computation | async-start | bytes 2097152 | tf_op jit(solution)/shard_map/all_to_all | solution.py:223
  42.2 2.5 %subtract_convert_fusion = (bf16[8,128,1024]{2,1,0:T(8,128)(2,1)S(1)}, bf16[8,128,1024]{2,1,0:T(8,128)(2,1)S(1)}) fusion(f32[128,1024]{1,0:T(8,128)} %get-tuple-element.54, f32[8,1024]{1,0:T(8,128)S(1)} %get-tuple-element.52, f32[128,1024]{1,0:T(8,128)} %get-tuple-element.53, f32[8,1024]{1,0:T(8,128)S(1)} %get-tuple-element.51), kind=kLoop, calls=%fused_computation.4 | loop fusion | flops 9437184 | bytes 5308416 | tf_op jit(solution)/shard_map/convert.23
  44.7 4.4 %multiply_subtract_fusion = (f32[8,128,1024]{2,1,0:T(8,128)}, f32[8,128,1024]{2,1,0:T(8,128)}) fusion(f32[128,1024]{1,0:T(8,128)S(1)} %copy-done.11, f32[8,1024]{1,0:T(8,128)S(1)} %get-tuple-element.46, f32[128,1024]{1,0:T(8,128)S(1)} %copy-done.10, f32[8,1024]{1,0:T(8,128)S(1)} %get-tuple-element.45), kind=kLoop, calls=%fused_computation.6 | loop fusion | flops 7340032 | bytes 9502720 | tf_op jit(solution)/shard_map/sub | solution.py:160
  49.1 4.4 %fusion.19 = f32[2048,512]{1,0:T(8,128)} fusion(bf16[1024,1024]{1,0:T(8,128)(2,1)S(1)} %bitcast.148, bf16[1024,1024]{1,0:T(8,128)(2,1)S(1)} %bitcast.145, f32[1024,512]{1,0:T(8,128)S(1)} %copy-done.24), kind=kOutput, calls=%fused_computation.45 | convolution fusion | flops 2156396544 | bytes 10485760 | tf_op jit(solution)/shard_map/dot_general | solution.py:175
  53.5 4.4 %fusion.17 = f32[2048,512]{1,0:T(8,128)} fusion(bf16[1024,512]{1,0:T(8,128)(2,1)S(1)} %bitcast.140, bf16[1024,1024]{1,0:T(8,128)(2,1)S(1)} %bitcast.149, bf16[1024,1024]{1,0:T(8,128)(2,1)S(1)} %bitcast.146), kind=kOutput, calls=%fused_computation.43 | convolution fusion | flops 2155872256 | bytes 9437184 | tf_op jit(solution)/shard_map/dot_general | solution.py:175
  58.0 9.6 %all-to-all-done = bf16[128,8,512]{2,0,1:T(8,128)(2,1)} async-done(((bf16[128,8,512]{2,0,1:T(8,128)(2,1)}), bf16[128,8,512]{2,0,1:T(8,128)(2,1)}, u32[]{:S(2)}, u32[]{:S(2)}) %all-to-all-start) | async-done | bytes 1048608 | tf_op jit(solution)/shard_map/all_to_all | solution.py:223
  67.6 5.0 %fusion.18 = f32[2048,512]{1,0:T(8,128)S(1)} fusion(bf16[1024,512]{1,0:T(8,128)(2,1)} %bitcast.9, bf16[1024,1024]{1,0:T(8,128)(2,1)} %bitcast.150, bf16[1024,1024]{1,0:T(8,128)(2,1)} %bitcast.147), kind=kOutput, calls=%fused_computation.44 | convolution fusion | flops 2155872256 | bytes 9437184 | tf_op jit(solution)/shard_map/dot_general | solution.py:175
  72.6 1.2 fusion.28
  73.8 2.2 fusion.30
  76.2 1.8 pad_maximum_fusion.1
  78.0 1.1 copy-done.3
  79.2 1.3 copy-done.5
  80.4 4.5 %add_convert_fusion.3 = bf16[1024,512]{1,0:T(8,128)(2,1)} fusion(bf16[1024,512]{1,0:T(8,128)(2,1)} %bitcast.9, bf16[2048,512]{1,0:T(8,128)(2,1)S(1)} %bitcast.151, f32[512]{0:T(512)S(1)} %bitcast.161, f32[1024,1024]{1,0:T(8,128)S(1)} %bitcast.136, f32[1024,1024]{1,0:T(8,128)S(1)} %bitcast.132), kind=kOutput, calls=%fused_computation.35 | convolution fusion | flops 2155872256 | bytes 12584960 | tf_op jit(solution)/shard_map/dot_general | solution.py:181
  85.0 3.3 %add_convert_fusion.1 = bf16[1024,512]{1,0:T(8,128)(2,1)} fusion(bf16[1024,512]{1,0:T(8,128)(2,1)S(1)} %bitcast.141, bf16[2048,512]{1,0:T(8,128)(2,1)S(1)} %bitcast.143, f32[512]{0:T(512)S(1)} %bitcast.162, f32[1024,1024]{1,0:T(8,128)S(1)} %bitcast.137, f32[1024,1024]{1,0:T(8,128)S(1)} %bitcast.133), kind=kOutput, calls=%fused_computation.32 | convolution fusion | flops 2155872256 | bytes 12584960 | tf_op jit(solution)/shard_map/dot_general | solution.py:181
  88.3 3.6 %all-to-all-start.3 = ((bf16[8,128,512]{2,1,0:T(8,128)(2,1)}), bf16[8,128,512]{2,1,0:T(8,128)(2,1)S(1)}, u32[]{:S(2)}, u32[]{:S(2)}) async-start(bf16[8,128,512]{2,1,0:T(8,128)(2,1)} %bitcast.154), calls=%async_computation.3 | async-start | bytes 2097152 | tf_op jit(solution)/shard_map/all_to_all | solution.py:252
  91.8 1.6 fusion.64
  93.4 1.6 fusion.63
  95.0 1.6 fusion.62
  96.6 1.6 fusion.61
  98.1 1.6 fusion.60
  99.7 1.6 fusion.59
  101.3 1.6 fusion.58
  102.8 1.6 fusion.57
  104.4 13.2 %all-to-all-done.3 = bf16[8,128,512]{2,1,0:T(8,128)(2,1)S(1)} async-done(((bf16[8,128,512]{2,1,0:T(8,128)(2,1)}), bf16[8,128,512]{2,1,0:T(8,128)(2,1)S(1)}, u32[]{:S(2)}, u32[]{:S(2)}) %all-to-all-start.3) | async-done | bytes 1048608 | tf_op jit(solution)/shard_map/all_to_all | solution.py:252
  117.6 4.2 %all-to-all-start.1 = ((bf16[8,128,512]{2,1,0:T(8,128)(2,1)}), bf16[8,128,512]{2,1,0:T(8,128)(2,1)}, u32[]{:S(2)}, u32[]{:S(2)}) async-start(bf16[8,128,512]{2,1,0:T(8,128)(2,1)} %fusion.57), calls=%async_computation.1 | async-start | bytes 2097152 | tf_op jit(solution)/shard_map/all_to_all | solution.py:247
  123.7 1.9 fusion.2
  125.6 21.9 %all-to-all-done.1 = bf16[8,128,512]{2,1,0:T(8,128)(2,1)} async-done(((bf16[8,128,512]{2,1,0:T(8,128)(2,1)}), bf16[8,128,512]{2,1,0:T(8,128)(2,1)}, u32[]{:S(2)}, u32[]{:S(2)}) %all-to-all-start.1) | async-done | bytes 1048608 | tf_op jit(solution)/shard_map/all_to_all | solution.py:247
  147.5 2.9 %convert_bitcast_fusion.5 = f32[128,8,512]{2,0,1:T(8,128)} fusion(bf16[8,128,512]{2,1,0:T(8,128)(2,1)} %all-to-all-done.1), kind=kLoop, calls=%fused_computation.27 | loop fusion | flops 524288 | bytes 3145728 | tf_op jit(solution)/shard_map/convert_element_type | solution.py:254
  150.4 2.9 %copy.24 = f32[128,8,512]{0,2,1:T(8,128)} copy(f32[128,8,512]{2,0,1:T(8,128)} %convert_bitcast_fusion.5) | data formatting | bytes 4194304 | tf_op jit(solution)/shard_map/convert_element_type | solution.py:254
  153.3 3.5 %fusion.7 = (bf16[128,4096]{0,1:T(8,128)(2,1)}, bf16[128,4096]{0,1:T(8,128)(2,1)}) fusion(bf16[1,128,4096]{1,2,0:T(8,128)(2,1)S(1)} %copy.25, f32[128,8,512]{0,2,1:T(8,128)} %copy.24, bf16[1,128,4096]{1,2,0:T(8,128)(2,1)S(1)} %copy.22), kind=kLoop, calls=%fused_computation.19 | loop fusion | flops 3145728 | bytes 6291456 | tf_op jit(solution)/shard_map/convert_element_type | solution.py:269
  157.2 1.2 collective-permute-start.2
  158.9 5.8 %multiply_reduce_fusion.1 = (f32[512]{0:T(512)}, f32[1024,512]{1,0:T(8,128)S(1)}) fusion(f32[1024,512]{1,0:T(8,128)} %fusion.12, f32[1024]{0:T(1024)S(1)} %negate_multiply_fusion, bf16[2048,512]{1,0:T(8,128)(2,1)S(1)} %bitcast.144, f32[1024,1024]{1,0:T(8,128)} %bitcast.135, f32[1024,1024]{1,0:T(8,128)S(1)} %bitcast.134), kind=kOutput, calls=%fused_computation.29 | convolution fusion | flops 2155347456 | bytes 14686208 | tf_op jit(solution)/shard_map/dot_general | solution.py:181
  164.7 3.3 %fusion.104 = (f32[64]{0:T(128)S(1)}, f32[1024,64]{0,1:T(8,128)S(1)}) fusion(f32[1024,64]{0,1:T(8,128)S(1)} %copy-done.17, f32[1,64,512]{2,1,0:T(8,128)S(1)} %copy-done, f32[1024,512]{1,0:T(8,128)S(1)} %get-tuple-element.60, f32[1024]{0:T(1024)S(1)} %iota_convert_fusion, f32[512]{0:T(512)S(1)} %bitcast.157), kind=kOutput, calls=%fused_computation.159 | convolution fusion | flops 404881344 | bytes 2758912 | tf_op jit(solution)/shard_map/fc,tc->ft/dot_general | solution.py:17
  168.4 36.3 %all-reduce = (f32[1,33,64]{2,1,0:T(8,128)S(1)}, f32[1,64]{1,0:T(1,128)}) all-reduce(f32[1,33,64]{2,1,0:T(8,128)S(1)} %convolution_bitcast_fusion, f32[1,64]{1,0:T(1,128)S(1)} %bitcast.160), channel_id=1, replica_groups=mesh['pipe'=4,'seq'=8] {'seq'}, use_global_device_ids=true, to_apply=%region_0.1 | all-reduce | flops 2176 | bytes 17408 | tf_op jit(solution)/shard_map/psum | solution.py:262
  205.3 2.2 multiply_reduce_fusion
  207.5 3.4 %fusion.23 = f32[1,64,512]{2,1,0:T(8,128)} fusion(f32[1024,64]{0,1:T(8,128)} %copy-done.16, f32[1024,512]{1,0:T(8,128)S(1)} %copy-done.23, f32[1024]{0:T(1024)S(1)} %iota_convert_fusion, f32[512]{0:T(512)S(1)} %bitcast.158), kind=kOutput, calls=%fused_computation.48 | convolution fusion | flops 404750336 | bytes 2496512 | tf_op jit(solution)/shard_map/ft,tc->fc/dot_general | solution.py:17
  210.9 2.3 %copy.29 = bf16[1,128,4096]{2,1,0:T(8,128)(2,1)} copy(bf16[1,128,4096]{1,2,0:T(8,128)(2,1)} %bitcast.40) | data formatting | bytes 2097152
  213.2 2.3 %copy.28 = bf16[1,128,4096]{2,1,0:T(8,128)(2,1)} copy(bf16[1,128,4096]{1,2,0:T(8,128)(2,1)} %bitcast.25) | data formatting | bytes 2097152
  (77 shorter events, 8.1 us)
Async XLA Ops:
  0.6 23.8 %copy-start = (f32[1,64,512]{2,1,0:T(8,128)S(1)}, f32[1,64,512]{2,1,0:T(8,128)}, u32[]{:S(2)}) copy-start(f32[1,64,512]{2,1,0:T(8,128)} %param.15) | copy-start | bytes 393220
  0.7 1.7 copy-start.15
  4.7 33.0 %all-to-all-start.2 = ((bf16[128,8,512]{2,0,1:T(8,128)(2,1)}), bf16[128,8,512]{2,0,1:T(8,128)(2,1)S(1)}, u32[]{:S(2)}, u32[]{:S(2)}) async-start(bf16[128,8,512]{2,0,1:T(8,128)(2,1)} %copy.26), calls=%async_computation.2 | async-start | bytes 2097152 | tf_op jit(solution)/shard_map/all_to_all | solution.py:224
  11.9 1.9 copy-start.19
  13.8 2.5 %copy-start.18 = (f32[1,33,64]{2,0,1:T(1,128)S(1)}, f32[1,33,64]{2,0,1:T(1,128)}, u32[]{:S(2)}) copy-start(f32[1,33,64]{2,0,1:T(1,128)} %param.13) | copy-start | bytes 25348
  13.8 2.5 %copy-start.20 = (f32[1,64]{1,0:T(1,128)S(1)}, f32[1,64]{1,0:T(1,128)}, u32[]{:S(2)}) copy-start(f32[1,64]{1,0:T(1,128)} %param.14) | copy-start | bytes 772
  18.3 6.1 %copy-start.16 = (f32[1024,64]{0,1:T(8,128)}, f32[1024,64]{0,1:T(8,128)S(1)}, u32[]{:S(2)}) copy-start(f32[1024,64]{0,1:T(8,128)S(1)} %get-tuple-element.55) | copy-start | bytes 786436
  37.7 47.3 %copy-start.6 = (bf16[128,8,512]{2,0,1:T(8,128)(2,1)}, bf16[128,8,512]{2,0,1:T(8,128)(2,1)S(1)}, u32[]{:S(2)}) copy-start(bf16[128,8,512]{2,0,1:T(8,128)(2,1)S(1)} %all-to-all-done.2) | copy-start | bytes 3145732
  37.7 29.9 %all-to-all-start = ((bf16[128,8,512]{2,0,1:T(8,128)(2,1)}), bf16[128,8,512]{2,0,1:T(8,128)(2,1)}, u32[]{:S(2)}, u32[]{:S(2)}) async-start(bf16[128,8,512]{2,0,1:T(8,128)(2,1)} %copy.23), calls=%async_computation | async-start | bytes 2097152 | tf_op jit(solution)/shard_map/all_to_all | solution.py:223
  42.1 2.6 %copy-start.10 = (f32[128,1024]{1,0:T(8,128)S(1)}, f32[128,1024]{1,0:T(8,128)}, u32[]{:S(2)}) copy-start(f32[128,1024]{1,0:T(8,128)} %get-tuple-element.47) | copy-start | bytes 1572868
  42.2 2.6 %copy-start.11 = (f32[128,1024]{1,0:T(8,128)S(1)}, f32[128,1024]{1,0:T(8,128)}, u32[]{:S(2)}) copy-start(f32[128,1024]{1,0:T(8,128)} %get-tuple-element.48) | copy-start | bytes 1572868
  44.7 8.8 %copy-start.13 = (bf16[8,128,1024]{2,1,0:T(8,128)(2,1)}, bf16[8,128,1024]{2,1,0:T(8,128)(2,1)S(1)}, u32[]{:S(2)}) copy-start(bf16[8,128,1024]{2,1,0:T(8,128)(2,1)S(1)} %get-tuple-element.43) | copy-start | bytes 6291460
  44.7 8.8 %copy-start.14 = (bf16[8,128,1024]{2,1,0:T(8,128)(2,1)}, bf16[8,128,1024]{2,1,0:T(8,128)(2,1)S(1)}, u32[]{:S(2)}) copy-start(bf16[8,128,1024]{2,1,0:T(8,128)(2,1)S(1)} %get-tuple-element.44) | copy-start | bytes 6291460
  44.7 4.4 %copy-start.24 = (f32[1024,512]{1,0:T(8,128)S(1)}, f32[1024,512]{1,0:T(8,128)}, u32[]{:S(2)}) copy-start(f32[1024,512]{1,0:T(8,128)} %fusion.12) | copy-start | bytes 6291460
  67.6 5.0 %copy-start.1 = (f32[2048,512]{1,0:T(8,128)S(1)}, f32[2048,512]{1,0:T(8,128)}, u32[]{:S(2)}) copy-start(f32[2048,512]{1,0:T(8,128)} %fusion.19) | copy-start | bytes 12582916
  67.6 5.0 %copy-start.2 = (f32[2048,512]{1,0:T(8,128)S(1)}, f32[2048,512]{1,0:T(8,128)}, u32[]{:S(2)}) copy-start(f32[2048,512]{1,0:T(8,128)} %fusion.17) | copy-start | bytes 12582916
  76.2 2.9 %copy-start.3 = (f32[8,128,1024]{2,1,0:T(8,128)S(1)}, f32[8,128,1024]{2,1,0:T(8,128)}, u32[]{:S(2)}) copy-start(f32[8,128,1024]{2,1,0:T(8,128)} %get-tuple-element.41) | copy-start | bytes 12582916
  76.2 4.2 %copy-start.5 = (f32[8,128,1024]{2,1,0:T(8,128)S(1)}, f32[8,128,1024]{2,1,0:T(8,128)}, u32[]{:S(2)}) copy-start(f32[8,128,1024]{2,1,0:T(8,128)} %get-tuple-element.42) | copy-start | bytes 12582916
  76.2 4.2 %copy-start.21 = (f32[1,512]{1,0:T(1,128)S(1)}, f32[1,512]{1,0:T(1,128)}, u32[]{:S(2)}) copy-start(f32[1,512]{1,0:T(1,128)} %param.17) | copy-start | bytes 6148
  88.3 29.3 %all-to-all-start.3 = ((bf16[8,128,512]{2,1,0:T(8,128)(2,1)}), bf16[8,128,512]{2,1,0:T(8,128)(2,1)S(1)}, u32[]{:S(2)}, u32[]{:S(2)}) async-start(bf16[8,128,512]{2,1,0:T(8,128)(2,1)} %bitcast.154), calls=%async_computation.3 | async-start | bytes 2097152 | tf_op jit(solution)/shard_map/all_to_all | solution.py:252
  117.6 29.9 %all-to-all-start.1 = ((bf16[8,128,512]{2,1,0:T(8,128)(2,1)}), bf16[8,128,512]{2,1,0:T(8,128)(2,1)}, u32[]{:S(2)}, u32[]{:S(2)}) async-start(bf16[8,128,512]{2,1,0:T(8,128)(2,1)} %fusion.57), calls=%async_computation.1 | async-start | bytes 2097152 | tf_op jit(solution)/shard_map/all_to_all | solution.py:247
  122.1 1.2 copy-start.8
  122.2 1.5 copy-start.9
  153.3 5.6 %copy-start.4 = (f32[8,128,1024]{2,1,0:T(8,128)S(1)}, f32[8,128,1024]{2,1,0:T(8,128)}, u32[]{:S(2)}) copy-start(f32[8,128,1024]{2,1,0:T(8,128)} %get-tuple-element.41) | copy-start | bytes 12582916
  153.3 5.6 %copy-start.12 = (bf16[2,1024,512]{2,1,0:T(8,128)(2,1)S(1)}, bf16[2,1024,512]{2,1,0:T(8,128)(2,1)}, u32[]{:S(2)}) copy-start(bf16[2,1024,512]{2,1,0:T(8,128)(2,1)} %get-tuple-element.62) | copy-start | bytes 6291460
  156.7 54.2 %collective-permute-start.3 = (bf16[128,4096]{0,1:T(8,128)(2,1)}, bf16[128,4096]{0,1:T(8,128)(2,1)}, u32[]{:S(2)}, u32[]{:S(2)}) collective-permute-start(bf16[128,4096]{0,1:T(8,128)(2,1)} %get-tuple-element.37), channel_id=1, source_target_pairs={{0,24},{8,0},{16,8},{24,16},{1,25},{9,1},{17,9},{25,17},{2,26},{10... | collective-permute-start | bytes 3145736 | tf_op jit(solution)/shard_map/ppermute | solution.py:13
  156.7 56.4 %collective-permute-start = (bf16[128,4096]{0,1:T(8,128)(2,1)}, bf16[128,4096]{0,1:T(8,128)(2,1)}, u32[]{:S(2)}, u32[]{:S(2)}) collective-permute-start(bf16[128,4096]{0,1:T(8,128)(2,1)} %get-tuple-element.38), channel_id=1, source_target_pairs={{0,8},{8,16},{16,24},{24,0},{1,9},{9,17},{17,25},{25,1},{2,10},{10... | collective-permute-start | bytes 3145736 | tf_op jit(solution)/shard_map/ppermute | solution.py:13
  157.2 58.2 %collective-permute-start.2 = (bf16[128,4096]{1,0:T(8,128)(2,1)}, bf16[128,4096]{1,0:T(8,128)(2,1)S(1)}, u32[]{:S(2)}, u32[]{:S(2)}) collective-permute-start(bf16[128,4096]{1,0:T(8,128)(2,1)} %get-tuple-element.39), channel_id=1, source_target_pairs={{0,24},{8,0},{16,8},{24,16},{1,25},{9,1},{17,9},{25,17},{2,26},{10... | collective-permute-start | bytes 3145736 | tf_op jit(solution)/shard_map/ppermute | solution.py:13
  158.5 57.0 %collective-permute-start.1 = (bf16[128,4096]{1,0:T(8,128)(2,1)}, bf16[128,4096]{1,0:T(8,128)(2,1)S(1)}, u32[]{:S(2)}, u32[]{:S(2)}) collective-permute-start(bf16[128,4096]{1,0:T(8,128)(2,1)} %get-tuple-element.40), channel_id=1, source_target_pairs={{0,24},{8,0},{16,8},{24,16},{1,25},{9,1},{17,9},{25,17},{2,26},{10... | collective-permute-start | bytes 3145736 | tf_op jit(solution)/shard_map/ppermute | solution.py:13
  158.9 5.8 %copy-start.17 = (f32[1024,64]{0,1:T(8,128)S(1)}, f32[1024,64]{0,1:T(8,128)}, u32[]{:S(2)}) copy-start(f32[1024,64]{0,1:T(8,128)} %get-tuple-element.56) | copy-start | bytes 786436
  164.7 3.7 %copy-start.22 = (f32[1024,512]{1,0:T(8,128)}, f32[1024,512]{1,0:T(8,128)S(1)}, u32[]{:S(2)}) copy-start(f32[1024,512]{1,0:T(8,128)S(1)} %get-tuple-element.60) | copy-start | bytes 6291460
  164.7 40.6 %copy-start.7 = (bf16[128,8,512]{2,0,1:T(8,128)(2,1)S(1)}, bf16[128,8,512]{2,0,1:T(8,128)(2,1)}, u32[]{:S(2)}) copy-start(bf16[128,8,512]{2,0,1:T(8,128)(2,1)} %copy-done.6) | copy-start | bytes 3145732
  204.7 2.8 %copy-start.23 = (f32[1024,512]{1,0:T(8,128)S(1)}, f32[1024,512]{1,0:T(8,128)}, u32[]{:S(2)}) copy-start(f32[1024,512]{1,0:T(8,128)} %copy-done.22) | copy-start | bytes 6291460
